TPU v7x, 128 devices: a whole 4x4x4 slice. The times are simulated.
128 devices in a mesh: grp: 8 (over y_lo, z), dev: 16 (over y_hi, x, core).
Axes of the slice: x: 4, y: 4 (y_hi: 2, y_lo: 2; y = y_hi * 2 + y_lo), z: 4, core: 2. Of those that a mesh axis runs over, the one named last changes fastest.
Arguments:
- queries: bfloat16 [131072, 2048], P(('grp', 'dev')), may hold values from -48 to 48
- key_rows: bfloat16 [131072, 2048], P(('grp', 'dev')), may hold values from -6 to 6
- value_rows: bfloat16 [131072, 2048], P(('grp', 'dev')), may hold values from -6 to 6
Outputs:
- attended: bfloat16 [131072, 2048], P(('grp', 'dev'))
All inputs are finite; a program needn't handle non-finite values.
Results may differ from a plain program's by a relative error of at most 0.0026.
Values may be sent and summed in bfloat16 or wider, within the bound.
A program may use at most 256 MiB of HBM per device.

v0:
```python
import math

import jax
import jax.numpy as jnp
import numpy as np
from jax import lax
from jax.sharding import PartitionSpec as P

H = 16


def attend(query_rows, key_part, value_part):
    score_scale = 1.0 / math.sqrt(query_rows.shape[-1])
    scores = (
        jnp.einsum("qhe,khe->hqk", query_rows, key_part, preferred_element_type=jnp.float32)
        * score_scale
    )
    maxima = jnp.max(scores, axis=2)
    weights = jnp.exp(scores - maxima[:, :, None])
    totals = jnp.sum(weights, axis=2)
    summed = jnp.einsum(
        "hqk,khe->qhe", weights.astype(jnp.bfloat16), value_part, preferred_element_type=jnp.float32
    )
    return (maxima.T, totals.T, summed)


def start_state(query_rows):
    row_count, head_count, head_width = query_rows.shape
    return (
        jnp.full((row_count, head_count), -jnp.inf, jnp.float32),
        jnp.zeros((row_count, head_count), jnp.float32),
        jnp.zeros((row_count, head_count, head_width), jnp.float32),
    )


def folder(query_rows, state_now, shard_piece):
    score_scale = 1.0 / math.sqrt(query_rows.shape[-1])
    maxima, totals, summed = state_now
    key_part, value_part = shard_piece
    scores = (
        jnp.einsum("qhe,khe->hqk", query_rows, key_part, preferred_element_type=jnp.float32)
        * score_scale
    )
    raised = jnp.maximum(maxima, jnp.max(scores, axis=2).T)
    weights = jnp.exp(scores - raised.T[:, :, None])
    shrink = jnp.exp(maxima - raised)
    totals = totals * shrink + jnp.sum(weights, axis=2).T
    summed = summed * shrink[:, :, None] + jnp.einsum(
        "hqk,khe->qhe", weights.astype(jnp.bfloat16), value_part, preferred_element_type=jnp.float32
    )
    return (raised, totals, summed)


def picked_rows(source, dilation):
    head_ids = np.arange(source.shape[1])
    shaped = source.reshape(source.shape[0] // dilation, dilation, source.shape[1], source.shape[2])
    return shaped[:, head_ids % dilation, head_ids, :]


def gap_between(maxima, totals, summed, dilation):
    head_count = maxima.shape[1]
    select_mask = jnp.asarray(
        np.arange(dilation)[:, None] == (np.arange(head_count) % dilation)[None, :]
    )
    full_max = jnp.where(select_mask[None], maxima[:, None, :], -jnp.inf).reshape(-1, head_count)
    full_tot = jnp.where(select_mask[None], totals[:, None, :], 0.0).reshape(-1, head_count)
    full_sum = jnp.where(select_mask[None, :, :, None], summed[:, None], 0.0).reshape(
        -1, head_count, summed.shape[2]
    )
    return (full_max, full_tot, full_sum)


def combine(branch_list):
    highest = branch_list[0][0]
    for branch in branch_list[1:]:
        highest = jnp.maximum(highest, branch[0])
    numerator = jnp.zeros_like(branch_list[0][2])
    denominator = jnp.zeros_like(branch_list[0][1])
    for branch in branch_list:
        factor = jnp.exp(branch[0] - highest)
        denominator = denominator + branch[1] * factor
        numerator = numerator + branch[2] * factor[:, :, None]
    return numerator / denominator[:, :, None]


def body(queries, key_rows, value_rows):
    tok_rows = queries.shape[0]
    head_width = queries.shape[1] // H
    processor_count = lax.axis_size("dev")
    group_number = lax.axis_size("grp")
    global_dilation = processor_count * group_number
    query_per_head = queries.reshape(tok_rows, H, head_width)
    key_per_head = key_rows.reshape(tok_rows, H, head_width)
    value_per_head = value_rows.reshape(tok_rows, H, head_width)
    block_rows = min(512, tok_rows)
    query_blocks = query_per_head.reshape(tok_rows // block_rows, block_rows, H, head_width)
    local_max, local_tot, local_sum = lax.map(
        lambda chosen: attend(chosen, key_per_head, value_per_head), query_blocks
    )
    local_part = (
        local_max.reshape(tok_rows, H),
        local_tot.reshape(tok_rows, H),
        local_sum.reshape(tok_rows, H, head_width),
    )
    group_query = picked_rows(query_per_head, processor_count)
    group_key = picked_rows(key_per_head, processor_count)
    group_value = picked_rows(value_per_head, processor_count)
    global_query = picked_rows(query_per_head, global_dilation)
    global_key = picked_rows(key_per_head, global_dilation)
    global_value = picked_rows(value_per_head, global_dilation)
    global_portion = folder(
        global_query,
        start_state(global_query),
        (
            lax.all_gather(global_key, ("grp", "dev"), axis=0, tiled=True),
            lax.all_gather(global_value, ("grp", "dev"), axis=0, tiled=True),
        ),
    )
    group_portion = folder(
        group_query,
        start_state(group_query),
        (
            lax.all_gather(group_key, "dev", axis=0, tiled=True),
            lax.all_gather(group_value, "dev", axis=0, tiled=True),
        ),
    )
    result = combine(
        [
            local_part,
            gap_between(group_portion[0], group_portion[1], group_portion[2], processor_count),
            gap_between(global_portion[0], global_portion[1], global_portion[2], global_dilation),
        ]
    )
    return result.reshape(tok_rows, H * head_width).astype(jnp.bfloat16)


def solution(mesh):
    in_specs = (P(("grp", "dev"), None), P(("grp", "dev"), None), P(("grp", "dev"), None))
    out_specs = P(("grp", "dev"), None)
    return jax.shard_map(body, mesh=mesh, in_specs=in_specs, out_specs=out_specs, check_vma=False)
```

profile of v0, /device:TPU:1, one launch (start us, length us, event | category | flops | bytes accessed | tf_op | source)
XLA Modules:
  0.0 651.3 jit_solution(3880444532441547648)
XLA Ops:
  34.4 9.0 %copy.63 = bf16[8,128,16,128]{3,0,2,1:T(8,128)(2,1)} copy(bf16[8,128,16,128]{3,2,1,0:T(8,128)(2,1)} %bitcast.202) | data formatting | bytes 8388608 | tf_op jit(solution)/shard_map/reshape;reshape | solution.py:56
  47.1 9.1 %copy.70 = bf16[8,128,16,128]{3,0,2,1:T(8,128)(2,1)} copy(bf16[8,128,16,128]{3,2,1,0:T(8,128)(2,1)} %bitcast.200) | data formatting | bytes 8388608 | tf_op jit(solution)/shard_map/reshape;reshape | solution.py:56
  59.6 6.4 copy.53
  66.1 6.4 copy.54
  78.1 6.4 copy.56
  84.5 6.4 copy.57
  90.9 115.2 %while.14 = (s32[]{:T(128)}, f32[2,512,16]{1,0,2:T(2,128)S(1)}, f32[2,512,16]{1,0,2:T(2,128)S(1)}, f32[2,512,16,128]{3,2,1,0:T(8,128)}, bf16[2,512,16,128]{3,2,1...) while((s32[]{:T(128)}, f32[2,512,16]{1,0,2:T(2,128)S(1)}, ...), condition=%wide.region_3.4_spmd, body=%wide.region_0.3_spmd.sunk | while | flops 4362059776 | bytes 145096848 | solution.py:97
  94.8 14.8 %multiply_reduce_fusion.3 = (f32[16,512]{1,0:T(8,128)S(1)}, f32[16,512,1024]{2,1,0:T(8,128)}) fusion(bf16[1024,16,128]{2,0,1:T(8,128)(2,1)S(1)} %copy-done, bf16[1,512,16,128]{3,2,1,0:T(8,128)(2,1)} %constant_dynamic-slice_fusion.2), kind=kOutput, calls=%fused_computation.7.clone.1 | convolution fusion | flops 2164252672 | bytes 39878656 | tf_op jit(solution)/shard_map/while/body/eval_jaxpr/qhe,khe->hqk/dot_general | solution.py:15
  109.8 14.4 %fusion.60 = f32[16,512]{1,0:T(8,128)S(1)} fusion(f32[16,512,1024]{2,1,0:T(8,128)} %get-tuple-element.135, f32[16,512]{1,0:T(8,128)S(1)} %get-tuple-element.134), kind=kLoop, calls=%fused_computation.9.clone.1 | loop fusion | flops 25157632 | bytes 33619968 | tf_op jit(solution)/shard_map/while/body/eval_jaxpr/reduce_sum | solution.py:20
  124.5 17.8 %fusion.61 = f32[1,512,16,128]{3,1,2,0:T(8,128)} fusion(bf16[1024,16,128]{2,0,1:T(8,128)(2,1)} %get-tuple-element.160, f32[16,512,1024]{2,1,0:T(8,128)} %get-tuple-element.135, f32[16,512]{1,0:T(8,128)S(1)} %get-tuple-element.134), kind=kOutput, calls=%fused_computation.14.clone.1 | convolution fusion | flops 2172649472 | bytes 41975808 | tf_op jit(solution)/shard_map/while/body/eval_jaxpr/hqk,khe->qhe/dot_general | solution.py:21
  142.3 6.7 %copy_dynamic-update-slice_fusion.2 = f32[2,512,16,128]{3,2,1,0:T(8,128)} fusion(f32[2,512,16,128]{3,2,1,0:T(8,128)} %get-tuple-element.148, s32[]{:T(128)S(6)} %copy.162, f32[1,512,16,128]{3,1,2,0:T(8,128)} %fusion.61), kind=kLoop, calls=%fused_computation.13.clone.1 | loop fusion | bytes 8388612 | tf_op jit(solution)/shard_map/while/body/jit(dynamic_update_index_in_dim)/dynamic_update_slice | solution.py:97
  152.4 14.8 %multiply_reduce_fusion.3 = (f32[16,512]{1,0:T(8,128)S(1)}, f32[16,512,1024]{2,1,0:T(8,128)}) fusion(bf16[1024,16,128]{2,0,1:T(8,128)(2,1)S(1)} %copy-done, bf16[1,512,16,128]{3,2,1,0:T(8,128)(2,1)} %constant_dynamic-slice_fusion.2), kind=kOutput, calls=%fused_computation.7.clone.1 | convolution fusion | flops 2164252672 | bytes 39878656 | tf_op jit(solution)/shard_map/while/body/eval_jaxpr/qhe,khe->hqk/dot_general | solution.py:15
  167.4 14.3 %fusion.60 = f32[16,512]{1,0:T(8,128)S(1)} fusion(f32[16,512,1024]{2,1,0:T(8,128)} %get-tuple-element.135, f32[16,512]{1,0:T(8,128)S(1)} %get-tuple-element.134), kind=kLoop, calls=%fused_computation.9.clone.1 | loop fusion | flops 25157632 | bytes 33619968 | tf_op jit(solution)/shard_map/while/body/eval_jaxpr/reduce_sum | solution.py:20
  182.0 17.4 %fusion.61 = f32[1,512,16,128]{3,1,2,0:T(8,128)} fusion(bf16[1024,16,128]{2,0,1:T(8,128)(2,1)} %get-tuple-element.160, f32[16,512,1024]{2,1,0:T(8,128)} %get-tuple-element.135, f32[16,512]{1,0:T(8,128)S(1)} %get-tuple-element.134), kind=kOutput, calls=%fused_computation.14.clone.1 | convolution fusion | flops 2172649472 | bytes 41975808 | tf_op jit(solution)/shard_map/while/body/eval_jaxpr/hqk,khe->qhe/dot_general | solution.py:21
  199.4 6.6 %copy_dynamic-update-slice_fusion.2 = f32[2,512,16,128]{3,2,1,0:T(8,128)} fusion(f32[2,512,16,128]{3,2,1,0:T(8,128)} %get-tuple-element.148, s32[]{:T(128)S(6)} %copy.162, f32[1,512,16,128]{3,1,2,0:T(8,128)} %fusion.61), kind=kLoop, calls=%fused_computation.13.clone.1 | loop fusion | bytes 8388612 | tf_op jit(solution)/shard_map/while/body/jit(dynamic_update_index_in_dim)/dynamic_update_slice | solution.py:97
  206.1 9.0 %copy.62 = bf16[8,128,16,128]{3,0,2,1:T(8,128)(2,1)} copy(bf16[8,128,16,128]{3,2,1,0:T(8,128)(2,1)} %bitcast.197) | data formatting | bytes 8388608 | tf_op jit(solution)/shard_map/reshape;reshape | solution.py:56
  218.4 6.9 %copy.60 = bf16[64,16,16,128]{3,0,2,1:T(8,128)(2,1)} copy(bf16[64,16,16,128]{3,2,1,0:T(8,128)(2,1)} %bitcast.198) | data formatting | bytes 8388608 | tf_op jit(solution)/shard_map/reshape;reshape | solution.py:56
  241.6 102.9 %all-gather.7.cloned.1.call-done = bf16[1024,16,128]{2,0,1:T(8,128)(2,1)} async-done(((bf16[8,16,128]{2,0,1:T(8,128)(2,1)}), bf16[1024,16,128]{2,0,1:T(8,128)(2,1)}) %all-gather.7.cloned.1.call-update) | async-done | bytes 4194320 | tf_op jit(solution)/shard_map/all_gather | solution.py:115
  348.9 201.5 %all-gather.11.cloned.1.call-done = bf16[1024,16,128]{2,0,1:T(8,128)(2,1)} async-done(((bf16[8,16,128]{2,0,1:T(8,128)(2,1)}), bf16[1024,16,128]{2,0,1:T(8,128)(2,1)}) %all-gather.11.cloned.1.call-update) | async-done | bytes 4194320 | tf_op jit(solution)/shard_map/all_gather | solution.py:116
  559.7 6.0 mul.91
  569.5 6.0 mul.87
  585.2 6.9 %broadcast_in_dim.228 = pred[1024,16,128]{2,1,0:T(8,128)(4,1)S(1)} broadcast(pred[1024,16]{1,0:T(8,128)(4,1)S(1)} %copy.69), dimensions={0,1} | broadcast | bytes 2113536 | tf_op jit(solution)/shard_map/jit(_where)/broadcast_in_dim | solution.py:67
  592.1 6.9 %broadcast_in_dim.219 = pred[1024,16,128]{2,1,0:T(8,128)(4,1)S(1)} broadcast(pred[1024,16]{1,0:T(8,128)(4,1)S(1)} %copy.65), dimensions={0,1} | broadcast | bytes 2113536 | tf_op jit(solution)/shard_map/jit(_where)/broadcast_in_dim | solution.py:67
  599.0 45.3 %fusion.11 = bf16[1024,2048]{1,0:T(8,128)(2,1)} fusion(f32[128,8,16,128]{3,2,1,0:T(8,128)} %bitcast.203, f32[128,8,16,128]{3,2,1,0:T(8,128)} %bitcast.204, f32[128,8,16,128]{3,2,1,0:T(8,128)} %bitcast.205, f32[128,8,16,128]{3,2,1,0:T(8,128)} %bitcast.206, f32[128,8,16,128]{3,2,1,0:T(8,128)} %bitcast.207, f32[128,8,16,128]{3,2,1,0:T(8,128)} %bitcast.208, ...), kind=kLoop, calls=%fused_computation.20 | loop fusion | flops 18874368 | bytes 67108864 | tf_op jit(solution)/shard_map/convert_element_type | solution.py:134
  (91 shorter events, 94.9 us)
Async XLA Ops:
  6.5 222.2 %all-gather.5.cloned.1.call-start = ((), (), s32[]{:S(2)}) async-start(), calls=%async_computation | async-start | bytes 4456448 | tf_op jit(solution)/shard_map/all_gather | solution.py:123
  6.5 24.1 %copy-start.4 = (s32[16]{0:T(128)}, s32[16]{0:T(128)S(1)}, u32[]{:S(2)}) copy-start(s32[16]{0:T(128)S(1)} %fusion.40) | copy-start | bytes 196
  10.1 2.0 copy-start.3
  20.3 216.1 %all-gather.9.cloned.1.call-start = ((), (), s32[]{:S(2)}) async-start(), calls=%async_computation.2 | async-start | bytes 4456448 | tf_op jit(solution)/shard_map/all_gather | solution.py:124
  24.0 2.0 copy-start.2
  34.1 310.4 %all-gather.7.cloned.1.call-start = ((), (), s32[]{:S(2)}) async-start(), calls=%async_computation.1 | async-start | bytes 4227072 | tf_op jit(solution)/shard_map/all_gather | solution.py:115
  43.4 12.8 %copy-start.6 = (s32[16]{0:T(128)}, s32[16]{0:T(128)S(1)}, u32[]{:S(2)}) copy-start(s32[16]{0:T(128)S(1)} %fusion.42) | copy-start | bytes 196
  46.8 503.6 %all-gather.11.cloned.1.call-start = ((), (), s32[]{:S(2)}) async-start(), calls=%async_computation.3 | async-start | bytes 4227072 | tf_op jit(solution)/shard_map/all_gather | solution.py:116
  91.3 3.5 copy-start
  149.0 3.5 copy-start
  206.1 9.1 %copy-start.7 = (s32[16]{0:T(128)S(1)}, s32[16]{0:T(128)}, u32[]{:S(2)}) copy-start(s32[16]{0:T(128)} %copy-done.6) | copy-start | bytes 196
  206.1 11.9 %copy-start.8 = (pred[16,16]{0,1:T(8,128)(4,1)S(1)}, pred[16,16]{0,1:T(8,128)(4,1)}, u32[]{:S(2)}) copy-start(pred[16,16]{0,1:T(8,128)(4,1)} %constant.15.clone) | copy-start | bytes 772
  218.3 6.9 %copy-start.5 = (s32[16]{0:T(128)S(1)}, s32[16]{0:T(128)}, u32[]{:S(2)}) copy-start(s32[16]{0:T(128)} %copy-done.4) | copy-start | bytes 196
  218.4 9.7 %copy-start.9 = (pred[128,16]{0,1:T(8,128)(4,1)S(1)}, pred[128,16]{0,1:T(8,128)(4,1)}, u32[]{:S(2)}) copy-start(pred[128,16]{0,1:T(8,128)(4,1)} %constant.17.clone) | copy-start | bytes 6148
  232.5 2.0 copy-start.1
Sparse Core Ops, SparseCore 0:
  20.4 59.6 all-gather.4
  82.6 54.8 all-gather.8
  139.1 205.3 all-gather.6
  346.0 204.3 all-gather.10
where the time goes:
time: 658 us; the launch traced here: 651 us
  waiting for transfers between devices  305 us (46%)
  local copies, waits for them, and re-layouts  177 us (27%)
  matrix products  79.8 us (12%)
  other arithmetic  75.2 us (11%)
  between operations  13.9 us (2%)
    all_gather x1, waiting for transfers between devices, body(): lax.all_gather(global_value, ('grp', 'dev'), axis=0, tiled=True)  202 us
    all_gather x1, waiting for transfers between devices, body(): lax.all_gather(global_key, ('grp', 'dev'), axis=0, tiled=True)  103 us
    convert_element_type x1, other arithmetic, body(): return result.reshape(tok_rows, H * head_width).astype(jnp.bfloat16)  45.3 us
    another operation x6, local copies, waits for them, and re-layouts, picked_rows(): source.reshape(source.shape[0] // dilation, dilation, source.shape[1], so...  43.3 us
    dot_general x2, matrix products, attend(): jnp.einsum('hqk,khe->qhe', weights.astype(jnp.bfloat16), value_part, pref...  35.2 us
    unnamed x26, local copies, waits for them, and re-layouts  31.7 us
    dot_general x2, matrix products, attend(): jnp.einsum('qhe,khe->hqk', query_rows, key_part, preferred_element_type=j...  29.6 us
    reduce_sum x2, other arithmetic, attend(): totals = jnp.sum(weights, axis=2)  28.8 us
  transfers between devices with their start and end apart: 4, of which 2 were waited for; matrix products, arithmetic and copies ran while one was open for 34% of the time, Pallas kernels for 0%

commit v1 on v0

v1 whole, which is shorter than its diff:
```python
import functools
import math

import jax
import jax.numpy as jnp
from jax import lax
from jax.experimental import pallas as pl
from jax.experimental.pallas import tpu as pltpu
from jax.sharding import PartitionSpec as P

H = 16
HD = 128
TQ = 256
MESH = pl.DeviceIdType.MESH
SCALE2 = math.log2(math.e) / math.sqrt(HD)
BF = jnp.bfloat16
F32 = jnp.float32


def scores_of(query_tile, key_part):
    return lax.dot_general(
        query_tile, key_part, (((1,), (1,)), ((), ())), preferred_element_type=F32
    )


def weigh(scores, value_ones):
    maxima = jnp.max(scores, axis=1, keepdims=True)
    weights = jnp.exp2((scores - maxima) * SCALE2).astype(BF)
    both = jnp.dot(weights, value_ones, preferred_element_type=F32)
    summed, totals = both[:, :HD], both[:, HD:]
    return summed / totals, maxima * SCALE2 + jnp.log2(totals)


def attend(load_query, key_part, value_part, rows, save):
    value_ones = jnp.concatenate([value_part, jnp.ones_like(value_part)], axis=1)
    tiles = rows // TQ
    scores = scores_of(load_query(0), key_part)
    for tile in range(tiles):
        later = scores_of(load_query(tile + 1), key_part) if tile + 1 < tiles else None
        save(tile, *weigh(scores, value_ones))
        scores = later


def merge(one, log_one, two, log_two):
    high = jnp.maximum(log_one, log_two)
    w_one, w_two = jnp.exp2(log_one - high), jnp.exp2(log_two - high)
    total = w_one + w_two
    return (one * w_one + two * w_two) / total, high + jnp.log2(total)


def kernel(
    n_grp, n_dev, split,
    q_hbm, k_hbm, v_hbm, out_hbm, mix_hbm,
    rows_in, rows_out, wide, wide_log, picked, staged, heads_in,
    glob_out, glob_in, back_out, back_log, back_in, back_log_in, own_sum, own_log, mix,
    load_sem, store_sem, mix_sem, go_sem, come_sem, glob_go, glob_come, back_go, back_come,
):
    grp, dev = lax.axis_index("grp"), lax.axis_index("dev")
    tok = q_hbm.shape[0]
    per = tok // n_dev
    chunk = tok // 4
    glob_rows = tok // n_grp
    sources = (q_hbm, k_hbm, v_hbm)
    order = (1, 2, 0)

    def load(which, part):
        rows = pl.ds(part * chunk, chunk)
        return pltpu.make_async_copy(
            sources[which].at[rows, :], rows_in.at[which, rows, :], load_sem.at[which, part]
        )

    for which in order:
        for part in range(4):
            load(which, part).start()

    barrier = pltpu.get_barrier_semaphore()
    for step in range(1, n_dev):
        pl.semaphore_signal(
            barrier, inc=1, device_id=(grp, lax.rem(dev + step, n_dev)), device_id_type=MESH
        )
    for step in range(1, n_grp):
        pl.semaphore_signal(
            barrier, inc=1, device_id=(lax.rem(grp + step, n_grp), dev), device_id_type=MESH
        )

    def send_rows(which, peer):
        return pltpu.make_async_remote_copy(
            src_ref=staged.at[which, peer], dst_ref=heads_in.at[which, dev],
            send_sem=go_sem.at[which, peer], recv_sem=come_sem.at[which, dev],
            device_id=(grp, peer), device_id_type=MESH,
        )

    def come_rows(which, peer):
        return pltpu.make_async_remote_copy(
            src_ref=staged.at[which, peer], dst_ref=heads_in.at[which, peer],
            send_sem=go_sem.at[which, peer], recv_sem=come_sem.at[which, peer],
            device_id=(grp, peer), device_id_type=MESH,
        )

    row_ids = lax.broadcasted_iota(jnp.int32, (1, n_dev, HD), 1).astype(F32).astype(BF)
    for number, which in enumerate(order):
        for part in range(4):
            load(which, part).wait()
            chosen = None
            for head in range(H):
                piece = rows_in[
                    which, part * chunk:(part + 1) * chunk, head * HD:(head + 1) * HD
                ].reshape(chunk // n_dev, n_dev, HD)
                if chosen is None:
                    chosen = piece
                else:
                    chosen = jnp.where(row_ids == jnp.asarray(head, BF), piece, chosen)
            picked[part * chunk:(part + 1) * chunk, :] = chosen.reshape(chunk, HD).astype(F32)
        for head in range(H):
            staged[which, head] = picked[pl.ds(head, per, stride=n_dev), :].astype(BF)
        if number == 0:
            pl.semaphore_wait(barrier, n_dev - 1 + n_grp - 1)
        heads_in[which, dev] = staged[which, dev]
        for step in range(1, n_dev):
            send_rows(which, lax.rem(dev + step, n_dev)).start()

    def store(head):
        columns = pl.ds(pl.multiple_of(head * HD, HD), HD)
        return pltpu.make_async_copy(
            rows_out.at[:, columns], out_hbm.at[:, columns], store_sem.at[head]
        )

    def local_heads(first, last):
        def one(head, carry):
            columns = pl.ds(pl.multiple_of(head * HD, HD), HD)

            def load_query(tile):
                return rows_in[0, pl.ds(tile * TQ, TQ), columns]

            def save(tile, normal, logs):
                rows = pl.ds(tile * TQ, TQ)
                rows_out[rows, columns] = normal.astype(BF)
                wide[rows, :] = normal
                wide_log[rows, :] = logs

            attend(load_query, rows_in[1, :, columns], rows_in[2, :, columns], tok, save)
            own_sum[head] = wide[pl.ds(head, per, stride=n_dev), :]
            own_log[head] = wide_log[pl.ds(head, per, stride=n_dev), :]
            store(head).start()
            return carry

        lax.fori_loop(first, last, one, 0)

    local_heads(0, split[0])

    for which in (1, 2):
        for step in range(1, n_dev):
            come_rows(which, lax.rem(dev + n_dev - step, n_dev)).wait_recv()
        picked[...] = heads_in[which].reshape(tok, HD).astype(F32)
        glob_out[which - 1] = picked[pl.ds(0, glob_rows, stride=n_grp), :].astype(BF)

    def send_glob(step):
        peer = lax.rem(grp + step, n_grp)
        return pltpu.make_async_remote_copy(
            src_ref=glob_out, dst_ref=glob_in.at[:, grp],
            send_sem=glob_go.at[peer], recv_sem=glob_come.at[grp],
            device_id=(peer, dev), device_id_type=MESH,
        )

    def come_glob(step):
        peer = lax.rem(grp + n_grp - step, n_grp)
        return pltpu.make_async_remote_copy(
            src_ref=glob_out, dst_ref=glob_in.at[:, peer],
            send_sem=glob_go.at[peer], recv_sem=glob_come.at[peer],
            device_id=(peer, dev), device_id_type=MESH,
        )

    for step in range(1, n_grp):
        send_glob(step).start()
    glob_in[:, grp] = glob_out[...]

    for step in range(1, n_dev):
        come_rows(0, lax.rem(dev + n_dev - step, n_dev)).wait_recv()

    def load_middle(tile):
        part = TQ // per
        return heads_in[0, tile * part:(tile + 1) * part].reshape(TQ, HD)

    def save_middle(tile, normal, logs):
        wide[tile * TQ:(tile + 1) * TQ, :] = normal
        wide_log[tile * TQ:(tile + 1) * TQ, :] = logs

    attend(
        load_middle, heads_in[1].reshape(tok, HD), heads_in[2].reshape(tok, HD), tok, save_middle
    )
    picked[...] = heads_in[0].reshape(tok, HD).astype(F32)

    for step in range(1, n_grp):
        come_glob(step).wait_recv()
    glob_query = picked[pl.ds(0, glob_rows, stride=n_grp), :].astype(BF)
    glob_value = glob_in[1].reshape(tok, HD)
    glob_normal, glob_log = weigh(
        scores_of(glob_query, glob_in[0].reshape(tok, HD)),
        jnp.concatenate([glob_value, jnp.ones_like(glob_value)], axis=1),
    )
    which_rows = pl.ds(0, glob_rows, stride=n_grp)
    both, both_log = merge(wide[which_rows, :], wide_log[which_rows, :], glob_normal, glob_log)
    wide[which_rows, :] = both
    wide_log[which_rows, :] = both_log
    back_out[...] = wide[...].astype(BF).reshape(n_dev, per, HD)
    lanes = lax.broadcasted_iota(jnp.int32, (1, 8, HD), 2) // (HD * 8 // per)
    logs = wide_log[...].reshape(n_dev, per // 8, 8, HD)
    packed = logs[:, 0]
    for turn in range(1, per // 8):
        packed = jnp.where(lanes == turn, logs[:, turn], packed)
    back_log[...] = packed

    def send_back(step):
        peer = lax.rem(dev + step, n_dev)
        return [
            pltpu.make_async_remote_copy(
                src_ref=src.at[peer], dst_ref=dst.at[dev],
                send_sem=back_go.at[number, peer], recv_sem=back_come.at[number, dev],
                device_id=(grp, peer), device_id_type=MESH,
            )
            for number, (src, dst) in enumerate(((back_log, back_log_in), (back_out, back_in)))
        ]

    def come_back(peer):
        return [
            pltpu.make_async_remote_copy(
                src_ref=src.at[peer], dst_ref=dst.at[peer],
                send_sem=back_go.at[number, peer], recv_sem=back_come.at[number, peer],
                device_id=(grp, peer), device_id_type=MESH,
            )
            for number, (src, dst) in enumerate(((back_log, back_log_in), (back_out, back_in)))
        ]

    for step in range(1, n_dev):
        for copy in send_back(step):
            copy.start()
    back_in[dev] = back_out[dev]
    back_log_in[dev] = back_log[dev]

    local_heads(split[0], H)

    for step in range(1, n_dev):
        for copy in come_back(lax.rem(dev + n_dev - step, n_dev)):
            copy.wait_recv()
    for head in range(H):
        lane_log = back_log_in[head]
        width = HD * 8 // per
        far_log = jnp.concatenate(
            [
                jnp.broadcast_to(lane_log[:, turn * width:turn * width + 1], (8, HD))
                for turn in range(per // 8)
            ],
            axis=0,
        )
        both, _ = merge(own_sum[head], own_log[head], back_in[head].astype(F32), far_log)
        mix[:, head * HD:(head + 1) * HD] = both.astype(BF)
    out_copy = pltpu.make_async_copy(mix, mix_hbm, mix_sem)
    out_copy.start()
    for which in order:
        for step in range(1, n_dev):
            send_rows(which, lax.rem(dev + step, n_dev)).wait_send()
    for step in range(1, n_grp):
        send_glob(step).wait_send()
    for step in range(1, n_dev):
        for copy in send_back(step):
            copy.wait_send()
    for head in range(H):
        store(head).wait()
    out_copy.wait()


def body(queries, key_rows, value_rows):
    tok, width = queries.shape
    n_dev, n_grp = lax.axis_size("dev"), lax.axis_size("grp")
    per = tok // n_dev
    any_spec = pl.BlockSpec(memory_space=pl.ANY)
    dma = pltpu.SemaphoreType.DMA
    local, mix = pl.pallas_call(
        functools.partial(kernel, n_grp, n_dev, (10,)),
        out_shape=(
            jax.ShapeDtypeStruct((tok, width), BF),
            jax.ShapeDtypeStruct((per, width), BF),
        ),
        in_specs=[any_spec] * 3,
        out_specs=(any_spec, any_spec),
        scratch_shapes=[
            pltpu.VMEM((3, tok, width), BF),
            pltpu.VMEM((tok, width), BF),
            pltpu.VMEM((tok, HD), F32),
            pltpu.VMEM((tok, HD), F32),
            pltpu.VMEM((tok, HD), F32),
            pltpu.VMEM((3, n_dev, per, HD), BF),
            pltpu.VMEM((3, n_dev, per, HD), BF),
            pltpu.VMEM((2, tok // n_grp, HD), BF),
            pltpu.VMEM((2, n_grp, tok // n_grp, HD), BF),
            pltpu.VMEM((n_dev, per, HD), BF),
            pltpu.VMEM((n_dev, 8, HD), F32),
            pltpu.VMEM((n_dev, per, HD), BF),
            pltpu.VMEM((n_dev, 8, HD), F32),
            pltpu.VMEM((H, per, HD), F32),
            pltpu.VMEM((H, per, HD), F32),
            pltpu.VMEM((per, width), BF),
            dma((3, 4)),
            dma((H,)),
            dma,
            dma((3, n_dev)),
            dma((3, n_dev)),
            dma((n_grp,)),
            dma((n_grp,)),
            dma((2, n_dev)),
            dma((2, n_dev)),
        ],
        compiler_params=pltpu.CompilerParams(
            collective_id=0, has_side_effects=True, vmem_limit_bytes=60 << 20
        ),
    )(queries, key_rows, value_rows)
    shape = (per, n_dev, H, HD)
    chosen = lax.broadcasted_iota(jnp.int32, (per, n_dev, width), 1) == (
        lax.broadcasted_iota(jnp.int32, (per, n_dev, width), 2) // HD
    )
    return jnp.where(
        chosen, mix[:, None, :], local.reshape(per, n_dev, width)
    ).reshape(tok, width)


def solution(mesh):
    spec = P(("grp", "dev"), None)
    return jax.shard_map(
        body, mesh=mesh, in_specs=(spec, spec, spec), out_specs=spec, check_vma=False
    )
```

time: 658 us -> 53.4 us (0.08); the launches traced: 651 us -> 53.3 us
  waiting for transfers between devices: 305 us -> 0 us
  local copies, waits for them, and re-layouts: 177 us -> 0.08 us
  matrix products: 79.8 us -> 0 us
  other arithmetic: 75.2 us -> 4.44 us
  Pallas kernels: 0 us -> 48.8 us
  between operations: 13.9 us -> 0.02 us
    all_gather x4 -> x0, waiting for transfers between devices: 304 us -> none  [the longest x1 202 us: body(): lax.all_gather(global_value, ('grp', 'dev'), axis=0, tiled=True)]
    dot_general x8 -> x0, matrix products: 79.8 us -> none  [the longest x2 35.2 us: attend(): jnp.einsum('hqk,khe->qhe', weights.astype(jnp.bfloat16), value_part, pref...]
    pallas_call x0 -> x1, Pallas kernels: none -> 48.8 us  [body(): pl.pallas_call(functools.partial(kernel, n_grp, n_dev, (10,)), out_shape=...]
    convert_element_type x1 -> x0, other arithmetic: 45.3 us -> none  [body(): return result.reshape(tok_rows, H * head_width).astype(jnp.bfloat16)]
    another operation x6 -> x0, local copies, waits for them, and re-layouts: 43.3 us -> none  [picked_rows(): source.reshape(source.shape[0] // dilation, dilation, source.shape[1], so...]
    unnamed x26 -> x0, local copies, waits for them, and re-layouts: 31.7 us -> none
    reduce_sum x4 -> x0, other arithmetic: 29.9 us -> none  [the longest x2 28.8 us: attend(): totals = jnp.sum(weights, axis=2)]
    broadcast_in_dim x15 -> x0, local copies, waits for them, and re-layouts: 23.5 us -> none  [the longest x4 21.5 us: gap_between(): jnp.where(select_mask[None, :, :, None], summed[:, None], 0.0)]
  transfers between devices with their start and end apart: 4 -> 0, of which waited for: 2 -> 0; matrix products, arithmetic and copies ran while one was open for 34% -> 0% of each run, Pallas kernels for 0% -> 0%
where the time goes in v1:
time: 53.4 us; the launch traced here: 53.3 us
  Pallas kernels  48.8 us (91%)
  other arithmetic  4.44 us (8%)
    pallas_call x1, Pallas kernels, body(): pl.pallas_call(functools.partial(kernel, n_grp, n_dev, (10,)), out_shape=...  48.8 us
    select_n x1, other arithmetic, body(): jnp.where(chosen, mix[:, None, :], local.reshape(per, n_dev, width))  4.43 us

profile of v1, /device:TPU:1, one launch (start us, length us, event | category | flops | bytes accessed | tf_op | source)
XLA Modules:
  0.0 53.3 jit_solution(9667980270654425820)
XLA Ops:
  0.0 0.1 iota.22
  0.1 48.8 %shard_map.37 = (bf16[1024,2048]{1,0:T(8,128)(2,1)}, bf16[64,2048]{1,0:T(8,128)(2,1)}) custom-call(bf16[1024,2048]{1,0:T(8,128)(2,1)} %q_hbm.1, bf16[1024,2048]{1,0:T(8,128)(2,1)} %k_hbm.1, bf16[1024,2048]{1,0:T(8,128)(2,1)} %v_hbm.1), custom_call_target="tpu_custom_call" | custom-call | tf_op jit(solution)/shard_map/pallas_call | solution.py:278
  48.9 4.4 %fusion = bf16[1024,2048]{1,0:T(8,128)(2,1)} fusion(bf16[1024,2048]{1,0:T(8,128)(2,1)} %get-tuple-element.8, s32[2048]{0:T(1024)S(1)} %get-tuple-element.9, s32[2048]{0:T(1024)S(1)} %get-tuple-element.10, s32[1024]{0:T(1024)S(1)} %iota.22, pred[2048]{0:T(1024)(128)(4,1)S(1)} %fusion.3, bf16[64,2048]{1,0:T(8,128)(2,1)} %get-tuple-element.7), kind=kLoop, calls=%fused_computation.1 | loop fusion | flops 6291456 | bytes 8673280 | tf_op jit(solution)/shard_map/jit(_where)/select_n | solution.py:321
  (3 shorter events, 0.0 us)
